TPU v7x, 32 devices: a whole 2x2x4 slice. The times are simulated.
32 devices in a mesh: row: 4 (over y, x), orb: 8 (over z, core).
Axes of the slice: x: 2, y: 2, z: 4, core: 2. Of those that a mesh axis runs over, the one named last changes fastest.
Arguments:
- integrals: bfloat16 [24, 1024, 5120], P('orb', 'row'), may hold values from -6 to 6
- tile_ids: int32 [8, 40], P('row'), may hold values from 0 to 127, as said below
- coefficients: bfloat16 [1024, 16384], P('orb'), may hold values from -0.078125 to 0.078125
- metric: float32 [24, 24], replicated, may hold values from -0.0078125 to 0.0078125
Outputs:
- exchange_columns: float32 [1024, 1024], P('orb', 'row')
Inputs may be any that keep to these rules, and one draw needn't show every extreme that they name: `tile_ids`: row block b covers basis functions b * 128 to b * 128 + 127. Each row lists 40 different column tiles (tile t covers basis functions t * 128 to t * 128 + 127); the first is the block's own tile b.
All inputs are finite; a program needn't handle non-finite values.
Results may differ from a plain program's by a relative error of at most 0.022.
Values may be sent and summed in bfloat16 or wider, within the bound.
A program may use at most 128 MiB of HBM per device.

v0:
```python
import functools

import jax
import jax.numpy as jnp
from jax import lax
from jax.experimental import pallas as pl
from jax.experimental.pallas import tpu as pltpu
from jax.sharding import PartitionSpec as P


def pick_kernel(count, tile, ids_ref, coef_ref, out_ref, sem):
    def begin(slot, carry):
        source = pl.ds(pl.multiple_of(ids_ref[slot] * tile, tile), tile)
        target = pl.ds(pl.multiple_of(slot * tile, tile), tile)
        pltpu.make_async_copy(coef_ref.at[:, source], out_ref.at[:, target], sem).start()
        return carry

    lax.fori_loop(0, count, begin, 0)
    pltpu.make_async_copy(coef_ref.at[:, pl.ds(0, count * tile)], out_ref, sem).wait()


def pick(coefficients, ids, tile):
    count = ids.shape[0]
    return pl.pallas_call(
        functools.partial(pick_kernel, count, tile),
        out_shape=jax.ShapeDtypeStruct((coefficients.shape[0], count * tile), coefficients.dtype),
        in_specs=[
            pl.BlockSpec(memory_space=pltpu.SMEM),
            pl.BlockSpec(memory_space=pl.ANY),
        ],
        out_specs=pl.BlockSpec(memory_space=pltpu.VMEM),
        scratch_shapes=[pltpu.SemaphoreType.DMA],
    )(ids, coefficients)


MESH = pl.DeviceIdType.MESH
CORES = 2
SPLIT = 2


def greet(peers):
    barrier = pltpu.get_barrier_semaphore()
    for peer in peers:
        pl.semaphore_signal(barrier, inc=1, device_id=peer, device_id_type=MESH)
    pl.semaphore_wait(barrier, len(peers))


def remote(source, target, send, recv, device):
    return pltpu.make_async_remote_copy(
        src_ref=source,
        dst_ref=target,
        send_sem=send,
        recv_sem=recv,
        device_id=device,
        device_id_type=MESH,
    )


def halves_kernel(dims, ids_ref, coef_ref, ints_ref, out_ref, *scratch):
    rows, chips, orb_local, tile, count, aux_local, blocks, part = dims
    quarter = orb_local // rows
    piece = quarter // SPLIT
    routes = [(d, s) for d in range(1, chips) for s in (1, -1)]
    scratch = list(scratch)
    raw = {}
    for route in range(len(routes)):
        for h in range(SPLIT):
            raw[route, h] = scratch.pop(0)
    own, first_rows, kept, staged, both, ready, ids_v, ids_s = scratch[:8]
    z_send, z_recv, p_send, p_recv, l_sem, i_send, i_recv, x_send, x_recv = scratch[8:]
    width = count * tile // blocks
    total = rows * chips
    row = lax.axis_index("row")
    orb = lax.axis_index("orb")
    chip = orb // CORES
    core = orb % CORES
    row_peers = [(lax.rem(row + t, rows), orb) for t in range(1, rows)]
    partner = (row, chip * CORES + 1 - core)
    me = row * chips + chip

    def place(k):
        other = lax.rem(me + k, total)
        return other, (other // chips, lax.rem(other, chips) * CORES + core)

    greet([place(k)[1] for k in range(1, total)] + [partner])

    def z_copy(route, h, device):
        return remote(
            first_rows.at[:, pl.ds(h * piece, piece), :] if routes[route][0] == 1 else raw[route - 2, h],
            raw[route, h],
            z_send.at[route, h],
            z_recv.at[route, h],
            device,
        )

    def towards(route):
        d, s = routes[route]
        there = chip + s
        start = chip - s * (d - 1)
        return there, (there >= 0) & (there < chips) & (start >= 0) & (start < chips)

    def origin(route):
        d, s = routes[route]
        there = chip - s * d
        return there, (there >= 0) & (there < chips)

    tiles = own.shape[0]

    def tile_copy(index, source_rows, target, sem):
        at = pl.ds(pl.multiple_of(index * tile, tile), tile)
        return pltpu.make_async_copy(coef_ref.at[source_rows, at], target.at[index], sem)

    def every(source_rows, target, sem, act):
        def some(index, carry):
            act(tile_copy(index, source_rows, target, sem))
            return carry

        lax.fori_loop(0, tiles, some, 0)

    quarter_rows = pl.ds(pl.multiple_of(row * quarter, quarter), quarter)
    all_rows = pl.ds(0, orb_local)
    every(quarter_rows, first_rows, l_sem.at[3], lambda copy: copy.start())
    id_copies = []
    for t in range(1, rows):
        id_copies.append(
            remote(ids_ref, ids_v.at[t], i_send.at[t], i_recv.at[t], row_peers[t - 1])
        )
        id_copies[-1].start()

    every(quarter_rows, first_rows, l_sem.at[3], lambda copy: copy.wait())
    for route in range(2):
        there, valid = towards(route)
        for h in range(SPLIT):

            @pl.when(valid)
            def _():
                z_copy(route, h, (row, there * CORES + core)).start()

    every(all_rows, own, l_sem.at[0], lambda copy: copy.start())
    swap = remote(ints_ref, both.at[1], i_send.at[0], i_recv.at[0], partner)
    swap.start()
    bring = pltpu.make_async_copy(ints_ref, both.at[0], l_sem.at[2])
    bring.start()
    first = pltpu.make_async_copy(ids_ref, ids_s.at[0], l_sem.at[1])
    first.start()
    first.wait()
    for t in range(1, rows):
        id_copies[t - 1].wait()
        move = pltpu.make_async_copy(ids_v.at[t], ids_s.at[t], l_sem.at[1])
        move.start()
        move.wait()

    def take(source, target, t):
        step = 8

        def some(block, carry):
            for k in range(step):
                slot = block * step + k
                at = pl.multiple_of(slot * tile, tile)
                target[:, pl.ds(at, tile)] = source[ids_s[t, 0, slot]]
            return carry

        lax.fori_loop(0, count // step, some, 0)

    def band(from_row, h):
        return pl.ds(pl.multiple_of(from_row * quarter + h * piece, piece), piece)

    def spread(from_row, came, h, t, device):
        k = lax.rem(came + chips - chip, chips) - 1
        return remote(
            staged.at[k, h, t - 1],
            kept.at[came, band(from_row, h), :],
            p_send.at[k, h, t],
            p_recv.at[k, h, t],
            device,
        )

    def handout(came, k):
        other, device = place(k)
        return remote(
            ready.at[came, other],
            out_ref.at[me, :, came],
            x_send.at[came, k],
            x_recv.at[came, k],
            device,
        )

    def keep(came):
        return pltpu.make_async_copy(
            ready.at[came, me], out_ref.at[me, :, came], x_send.at[came, 0]
        )

    def product(came):
        def one(step, carry):
            side = step // blocks
            block = step - side * blocks
            lhs = kept[came, :, pl.ds(pl.multiple_of(block * width, width), width)]
            at = pl.ds(pl.multiple_of(block * tile, tile), tile)
            rhs = both[side, :, at, :].reshape(aux_local * tile, width)
            result = lax.dot_general(
                lhs, rhs, (((1,), (1,)), ((), ())), preferred_element_type=jnp.float32
            )
            for p in range(aux_local):
                value = result[:, p * tile : (p + 1) * tile].astype(ready.dtype)
                ready[came, :, side * aux_local + p, :, at] = value.reshape(total, part, tile)
            return carry

        lax.fori_loop(0, CORES * blocks, one, 0)
        for k in range(1, total):
            handout(came, k).start()
        keep(came).start()

    every(all_rows, own, l_sem.at[0], lambda copy: copy.wait())
    take(own, kept.at[chip], 0)

    def pass_on(d):
        for h in range(SPLIT):
            for route in range(len(routes)):
                if routes[route][0] != d:
                    continue
                came, valid = origin(route)

                @pl.when(valid)
                def _():
                    z_copy(route, h, partner).wait_recv()
                    if d + 1 < chips:
                        there, onward = towards(route + 2)

                        @pl.when(onward)
                        def _():
                            z_copy(route + 2, h, (row, there * CORES + core)).start()

                    k = lax.rem(came + chips - chip, chips) - 1
                    for t in range(1, rows):
                        take(raw[route, h], staged.at[k, h, t - 1], t)
                        spread(row, came, h, t, row_peers[rows - t - 1]).start()
                    take(raw[route, h], kept.at[came, band(row, h), :], 0)

    def multiply(d):
        for route in range(len(routes)):
            if routes[route][0] != d:
                continue
            came, valid = origin(route)

            @pl.when(valid)
            def _():
                for h in range(SPLIT):
                    for t in range(1, rows):
                        source_row = lax.rem(row + t, rows)
                        spread(source_row, came, h, t, row_peers[0]).wait_recv()
                product(came)

    for d in range(1, chips):
        pass_on(d)
        if d == 1:
            bring.wait()
            swap.wait()
            product(chip)
        else:
            multiply(d - 1)
    multiply(chips - 1)

    for route in range(len(routes)):
        there, sent = towards(route)
        came, valid = origin(route)
        for h in range(SPLIT):

            @pl.when(sent)
            def _():
                z_copy(route, h, (row, there * CORES + core)).wait_send()

            @pl.when(valid)
            def _():
                for t in range(1, rows):
                    spread(row, came, h, t, row_peers[rows - t - 1]).wait_send()

    for came in range(chips):
        keep(came).wait()
        for k in range(1, total):
            handout(came, k).wait_send()
            other, device = place(total - k)
            remote(
                ready.at[came, me],
                out_ref.at[other, :, came],
                x_send.at[came, k],
                x_recv.at[came, k],
                device,
            ).wait_recv()


def halves_by_part(integrals, ids, coefficients, rows, orbs, blocks, count):
    chips = orbs // CORES
    orb_local, basis = coefficients.shape
    aux_local, local_rows, _ = integrals.shape
    tile = local_rows // blocks
    total = rows * chips
    part = orb_local // total
    piece = orb_local // rows // SPLIT
    routes = 2 * (chips - 1)
    dtype = coefficients.dtype
    scratch = [
        pltpu.VMEM((basis // tile, piece, tile), dtype) for _ in range(routes * SPLIT)
    ]
    scratch += [
        pltpu.VMEM((basis // tile, orb_local, tile), dtype),
        pltpu.VMEM((basis // tile, orb_local // rows, tile), dtype),
        pltpu.VMEM((chips, orb_local, count * tile), dtype),
        pltpu.VMEM((chips - 1, SPLIT, rows - 1, piece, count * tile), dtype),
        pltpu.VMEM((CORES,) + integrals.shape, dtype),
        pltpu.VMEM((chips, total, CORES * aux_local, part, local_rows), dtype),
        pltpu.VMEM((rows, 1, ids.shape[1]), jnp.int32),
        pltpu.SMEM((rows, 1, ids.shape[1]), jnp.int32),
        pltpu.SemaphoreType.DMA((routes, SPLIT)),
        pltpu.SemaphoreType.DMA((routes, SPLIT)),
        pltpu.SemaphoreType.DMA((chips - 1, SPLIT, rows)),
        pltpu.SemaphoreType.DMA((chips - 1, SPLIT, rows)),
        pltpu.SemaphoreType.DMA((4,)),
        pltpu.SemaphoreType.DMA((rows,)),
        pltpu.SemaphoreType.DMA((rows,)),
        pltpu.SemaphoreType.DMA((chips, total)),
        pltpu.SemaphoreType.DMA((chips, total)),
    ]
    dims = (rows, chips, orb_local, tile, count, aux_local, blocks, part)
    return pl.pallas_call(
        functools.partial(halves_kernel, dims),
        out_shape=jax.ShapeDtypeStruct(
            (total, CORES * aux_local, chips, part, local_rows), dtype
        ),
        in_specs=[pl.BlockSpec(memory_space=pltpu.VMEM)]
        + [pl.BlockSpec(memory_space=pl.ANY)] * 2,
        out_specs=pl.BlockSpec(memory_space=pl.ANY),
        scratch_shapes=scratch,
        compiler_params=pltpu.CompilerParams(
            collective_id=0, has_side_effects=True, vmem_limit_bytes=60 << 20
        ),
    )(ids, coefficients, integrals)


def finish_kernel(rows, chips, gram_ref, all_ref, out_ref, *scratch):
    part0, sum0, part1, sum1, part2, share, full, coef_ref = scratch[:8]
    send0, recv0, send1, recv1, send2, recv2, send3, recv3, l_sem = scratch[8:]
    window = pltpu.make_async_copy(
        all_ref.at[:, pl.ds(0, coef_ref.shape[1])], coef_ref, l_sem
    )
    window.start()
    row = lax.axis_index("row")
    orb = lax.axis_index("orb")
    chip = orb // CORES
    core = orb % CORES
    height = share.shape[0]
    half = height * chips
    partner = (row, chip * CORES + 1 - core)
    row_peers = [lax.rem(row + t, rows) for t in range(1, rows)]
    chip_peers = [lax.rem(chip + t, chips) for t in range(1, chips)]
    greet(
        [partner]
        + [(peer, orb) for peer in row_peers]
        + [(row, peer * CORES + core) for peer in chip_peers]
    )
    order = row_peers + [row]
    first = []
    for t, peer in enumerate(order):
        first.append(
            remote(
                gram_ref.at[peer, 1 - core], part0.at[peer], send0.at[t], recv0.at[t], partner
            )
        )
        first[-1].start()
    second = []
    for t, peer in enumerate(order):
        first[t].wait_recv()
        total = gram_ref[peer, core].astype(jnp.float32) + part0[peer].astype(jnp.float32)
        sum0[peer] = total.astype(sum0.dtype)
        if t < rows - 1:
            second.append(
                remote(sum0.at[peer], part1.at[t], send1.at[t], recv1.at[t], (peer, orb))
            )
            second[-1].start()
    for copy in second:
        copy.wait_recv()
    total = sum0[row].astype(jnp.float32)
    for t in range(rows - 1):
        total = total + part1[t].astype(jnp.float32)
    sum1[...] = total.astype(sum1.dtype).reshape(sum1.shape)
    third = []
    for t, peer in enumerate(chip_peers):
        device = (row, peer * CORES + core)
        third.append(remote(sum1.at[peer], part2.at[t], send2.at[t], recv2.at[t], device))
        third[-1].start()
    for copy in third:
        copy.wait_recv()
    total = sum1[chip].astype(jnp.float32)
    for t in range(chips - 1):
        total = total + part2[t].astype(jnp.float32)
    share[...] = total.astype(share.dtype)

    def block(from_core, from_chip):
        start = pl.multiple_of(from_core * half + from_chip * height, height)
        return full.at[pl.ds(start, height), :]

    fourth = [
        remote(share, block(core, chip), send3.at[0, 0], recv3.at[0, 0], partner)
    ]
    for t, peer in enumerate(chip_peers):
        device = (row, peer * CORES + core)
        fourth.append(
            remote(share, block(core, chip), send3.at[0, t + 1], recv3.at[0, t + 1], device)
        )
    for copy in fourth:
        copy.start()
    full[pl.ds(pl.multiple_of(core * half + chip * height, height), height), :] = share[...]
    passed = []
    for t in range(1, chips):
        source = lax.rem(chip + chips - t, chips)
        remote(
            share, block(core, source), send3.at[0, t], recv3.at[0, t], partner
        ).wait_recv()
        passed.append(
            remote(
                block(core, source),
                block(core, source),
                send3.at[1, t],
                recv3.at[1, t],
                partner,
            )
        )
        passed[-1].start()
    mine = pl.ds(pl.multiple_of(core * half, half), half)
    theirs = pl.ds(pl.multiple_of((1 - core) * half, half), half)
    window.wait()
    result = jnp.dot(coef_ref[:, mine], full[mine, :], preferred_element_type=jnp.float32)
    remote(share, block(1 - core, chip), send3.at[0, 0], recv3.at[0, 0], partner).wait_recv()
    for t in range(1, chips):
        source = lax.rem(chip + chips - t, chips)
        remote(
            block(core, source), block(1 - core, source), send3.at[1, t], recv3.at[1, t], partner
        ).wait_recv()
    out_ref[...] = result + jnp.dot(
        coef_ref[:, theirs], full[theirs, :], preferred_element_type=jnp.float32
    )
    for copy in first + second + third + fourth + passed:
        copy.wait_send()


def finish(gram, coefs, rows, chips):
    width = gram.shape[-1]
    half = gram.shape[2]
    height = half // chips
    dtype = gram.dtype
    return pl.pallas_call(
        functools.partial(finish_kernel, rows, chips),
        out_shape=jax.ShapeDtypeStruct((coefs.shape[0], width), jnp.float32),
        in_specs=[
            pl.BlockSpec(memory_space=pltpu.VMEM),
            pl.BlockSpec(memory_space=pl.ANY),
        ],
        out_specs=pl.BlockSpec(memory_space=pltpu.VMEM),
        scratch_shapes=[
            pltpu.VMEM((rows, half, width), dtype),
            pltpu.VMEM((rows, half, width), dtype),
            pltpu.VMEM((rows - 1, half, width), dtype),
            pltpu.VMEM((chips, height, width), dtype),
            pltpu.VMEM((chips - 1, height, width), dtype),
            pltpu.VMEM((height, width), dtype),
            pltpu.VMEM((CORES * half, width), dtype),
            pltpu.VMEM((coefs.shape[0], CORES * half), dtype),
            pltpu.SemaphoreType.DMA((rows,)),
            pltpu.SemaphoreType.DMA((rows,)),
            pltpu.SemaphoreType.DMA((rows,)),
            pltpu.SemaphoreType.DMA((rows,)),
            pltpu.SemaphoreType.DMA((chips,)),
            pltpu.SemaphoreType.DMA((chips,)),
            pltpu.SemaphoreType.DMA((CORES, chips)),
            pltpu.SemaphoreType.DMA((CORES, chips)),
            pltpu.SemaphoreType.DMA,
        ],
        compiler_params=pltpu.CompilerParams(collective_id=2, has_side_effects=True),
    )(gram, coefs)


def per_device(rows, orbs, integrals, tile_ids, coefficients, metric):
    aux_local, local_rows, kept_width = integrals.shape
    orb_local, basis_width = coefficients.shape
    block_count, kept_count = tile_ids.shape
    if orb_local % (16 * SPLIT * rows) or orb_local * CORES % (8 * rows * orbs) or block_count * kept_count % 8:
        return plain_device(rows, orbs, integrals, tile_ids, coefficients, metric)
    chips = orbs // CORES
    aux = aux_local * orbs
    window = local_rows * rows
    count = block_count * kept_count
    held = chips * orb_local
    part = held // (rows * chips)
    lanes = -(-count // 128) * 128
    ids = jnp.pad(tile_ids.reshape(1, count), ((0, 0), (0, lanes - count)))
    by_part = halves_by_part(integrals, ids, coefficients, rows, orbs, block_count, count)
    by_part = by_part.reshape(rows, aux, part, local_rows)
    core = lax.axis_index("orb") % CORES
    order = metric.reshape(chips, CORES, aux_local, chips, CORES, aux_local)
    order = jnp.where(core == 0, order, order[:, ::-1, :, :, ::-1, :]).reshape(aux, aux)
    mixed = jnp.einsum(
        "pq,rpjm->rqjm", order, by_part.astype(jnp.float32), precision=lax.Precision.HIGHEST
    ).astype(jnp.bfloat16)
    gram = jnp.einsum(
        "rqjm,sqjn->srmn", by_part, mixed, preferred_element_type=jnp.float32
    ).astype(jnp.bfloat16)
    gram = gram.reshape(rows, CORES, window // CORES, local_rows)
    return finish(gram, coefficients, rows, chips)


def plain_device(rows, orbs, integrals, tile_ids, coefficients, metric):
    aux_local, local_rows, kept_width = integrals.shape
    orb_local, basis_width = coefficients.shape
    block_count, kept_count = tile_ids.shape
    tile_rows = local_rows // block_count
    orbitals = orb_local * orbs
    aux = aux_local * orbs
    window = local_rows * rows
    part = orbitals // (rows * orbs)
    picked = pick(coefficients, tile_ids.reshape(block_count * kept_count), tile_rows)
    col_piece = lax.all_gather(picked, "orb", axis=0, tiled=True)
    slabs = integrals.reshape(aux_local, block_count, tile_rows, kept_width)
    halves = [
        jnp.einsum(
            "pmk,jk->pjm",
            slabs[:, b],
            col_piece[:, b * kept_width : (b + 1) * kept_width],
            preferred_element_type=jnp.float32,
        ).astype(jnp.bfloat16)
        for b in range(block_count)
    ]
    halves = jnp.concatenate(halves, axis=2)
    outgoing = halves.reshape(aux_local, rows * orbs, part, local_rows).transpose(1, 0, 2, 3)
    by_part = lax.all_to_all(outgoing, ("row", "orb"), split_axis=0, concat_axis=0, tiled=True)
    by_part = by_part.reshape(rows, aux, part, local_rows)
    mixed = jnp.einsum(
        "pq,rpjm->rqjm", metric, by_part.astype(jnp.float32), precision=lax.Precision.HIGHEST
    ).astype(jnp.bfloat16)
    gram = jnp.einsum(
        "rqjm,sqjn->rmsn", by_part, mixed, preferred_element_type=jnp.float32
    ).astype(jnp.bfloat16)
    gram = gram.reshape(orbs, window // orbs, rows, local_rows).transpose(2, 0, 1, 3)
    gram = gram.reshape(rows * window, local_rows)
    share = lax.psum_scatter(gram, ("row", "orb"), scatter_dimension=0, tiled=True)
    columns = lax.all_gather(share, "orb", axis=0, tiled=True)
    return jnp.dot(coefficients[:, :window], columns, preferred_element_type=jnp.float32)


def solution(mesh):
    return jax.shard_map(
        functools.partial(per_device, mesh.shape["row"], mesh.shape["orb"]),
        mesh=mesh,
        in_specs=(P("orb", "row", None), P("row", None), P("orb", None), P()),
        out_specs=P("orb", "row"),
        check_vma=False,
    )
```

profile of v0, /device:TPU:1, one launch (start us, length us, event | category | flops | bytes accessed | tf_op | source)
XLA Modules:
  0.0 179.2 jit_solution(5091482493730501172)
XLA Ops:
  0.0 0.8 reshape.15
  0.8 0.5 pad.4.ids_ref
  1.3 0.9 reshape.17
  2.2 0.2 rev.3
  2.4 0.2 reshape.20
  2.6 129.1 %shard_map.46 = bf16[16,6,4,8,256]{4,3,2,1,0:T(8,128)(2,1)} custom-call(s32[1,128]{1,0:T(1,128)} %pad.4.ids_ref, bf16[128,16384]{1,0:T(8,128)(2,1)} %all_ref.1, bf16[3,256,5120]{2,1,0:T(8,128)(2,1)} %ints_ref.1), custom_call_target="tpu_custom_call" | custom-call | tf_op jit(solution)/shard_map/pallas_call | solution.py:324
  131.6 0.0 copy-start
  131.6 3.4 %fusion.2 = bf16[4,32,256,24]{2,3,1,0:T(8,128)(2,1)S(1)} fusion(bf16[4,24,32,256]{3,2,1,0:T(8,128)(2,1)} %bitcast.23, f32[24,24,1,1]{1,0,2,3:T(8,128)S(1)} %reshape.20), kind=kOutput, calls=%fused_computation.3 | convolution fusion | flops 226492416 | bytes 3148032 | tf_op jit(solution)/shard_map/pq,rpjm->rqjm/dot_general | solution.py:500
  135.1 0.0 copy-done
  135.1 3.2 %bitcast_convert_fusion = bf16[4,256,4,256]{1,3,2,0:T(8,128)(2,1)} fusion(bf16[4,24,32,256,1]{3,2,1,0,4:T(8,128)(2,1)S(1)} %bitcast.24, bf16[4,32,256,24]{2,3,1,0:T(8,128)(2,1)S(1)} %fusion.2), kind=kOutput, calls=%fused_computation | convolution fusion | flops 1611661312 | bytes 5242880 | tf_op jit(solution)/shard_map/rqjm,sqjn->srmn/dot_general | solution.py:503
  138.3 39.3 %shard_map.47 = f32[128,256]{1,0:T(8,128)} custom-call(bf16[4,2,512,256]{3,2,1,0:T(8,128)(2,1)} %bitcast.25, bf16[128,16384]{1,0:T(8,128)(2,1)} %all_ref.1), custom_call_target="tpu_custom_call" | custom-call | tf_op jit(solution)/shard_map/pallas_call | solution.py:450
  177.6 1.6 copy.17
  (1 shorter events, 0.0 us)
Async XLA Ops:
  131.6 3.4 %copy-start = (bf16[16,6,4,8,256]{4,3,2,1,0:T(8,128)(2,1)S(1)}, bf16[16,6,4,8,256]{4,3,2,1,0:T(8,128)(2,1)}, u32[]{:S(2)}) copy-start(bf16[16,6,4,8,256]{4,3,2,1,0:T(8,128)(2,1)} %shard_map.46) | copy-start | bytes 4718596
where the time goes:
time: 180 us; the launch traced here: 179 us
  Pallas kernels  168 us (93%)
  matrix products  6.64 us (4%)
  local copies, waits for them, and re-layouts  4.09 us (2%)
    pallas_call x1, Pallas kernels, halves_by_part(): pl.pallas_call(functools.partial(halves_kernel, dims), out_shape=jax.Shap...  129 us
    pallas_call x1, Pallas kernels, finish(): pl.pallas_call(functools.partial(finish_kernel, rows, chips), out_shape=j...  39.3 us

commit v1 on v0

v1 whole, which is shorter than its diff:
```python
import functools

import jax
import jax.numpy as jnp
from jax import lax
from jax.experimental import pallas as pl
from jax.experimental.pallas import tpu as pltpu
from jax.sharding import PartitionSpec as P


def pick_kernel(count, tile, ids_ref, coef_ref, out_ref, sem):
    def begin(slot, carry):
        source = pl.ds(pl.multiple_of(ids_ref[slot] * tile, tile), tile)
        target = pl.ds(pl.multiple_of(slot * tile, tile), tile)
        pltpu.make_async_copy(coef_ref.at[:, source], out_ref.at[:, target], sem).start()
        return carry

    lax.fori_loop(0, count, begin, 0)
    pltpu.make_async_copy(coef_ref.at[:, pl.ds(0, count * tile)], out_ref, sem).wait()


def pick(coefficients, ids, tile):
    count = ids.shape[0]
    return pl.pallas_call(
        functools.partial(pick_kernel, count, tile),
        out_shape=jax.ShapeDtypeStruct((coefficients.shape[0], count * tile), coefficients.dtype),
        in_specs=[
            pl.BlockSpec(memory_space=pltpu.SMEM),
            pl.BlockSpec(memory_space=pl.ANY),
        ],
        out_specs=pl.BlockSpec(memory_space=pltpu.VMEM),
        scratch_shapes=[pltpu.SemaphoreType.DMA],
    )(ids, coefficients)


MESH = pl.DeviceIdType.MESH
CORES = 2
SPLIT = 2
OWNERS = 2


def greet(peers):
    barrier = pltpu.get_barrier_semaphore()
    for peer in peers:
        pl.semaphore_signal(barrier, inc=1, device_id=peer, device_id_type=MESH)
    pl.semaphore_wait(barrier, len(peers))


def remote(source, target, send, recv, device):
    return pltpu.make_async_remote_copy(
        src_ref=source,
        dst_ref=target,
        send_sem=send,
        recv_sem=recv,
        device_id=device,
        device_id_type=MESH,
    )


def exchange_kernel(dims, ids_ref, metric_ref, coef_ref, ints_ref, out_ref, *scratch):
    rows, chips, orb_local, tile, count, aux_local, blocks, part = dims
    piece = orb_local // rows // SPLIT
    group = piece * rows
    routes = [(d, s) for d in range(1, chips) for s in (1, -1)]
    scratch = list(scratch)
    raw = {}
    for route in range(len(routes)):
        for h in range(SPLIT):
            raw[route, h] = scratch.pop(0)
    own, first_rows, kept, staged, both, ready, ids_v, ids_s = scratch[:8]
    parts, weight, crossed, mixed, total_ref = scratch[8:13]
    gram, part0, sum0, part1, sum1, part2, share, full, window_ref = scratch[13:22]
    z_send, z_recv, p_send, p_recv, l_sem, i_send, i_recv, x_send, x_recv = scratch[22:31]
    q_send, q_recv = scratch[31:33]
    send0, recv0, send1, recv1, send2, recv2, send3, recv3 = scratch[33:]
    width = count * tile // blocks
    total = rows * chips
    owners = rows * OWNERS
    row = lax.axis_index("row")
    orb = lax.axis_index("orb")
    chip = orb // CORES
    core = orb % CORES
    row_peers = [(lax.rem(row + t, rows), orb) for t in range(1, rows)]
    partner = (row, chip * CORES + 1 - core)
    me = row * chips + chip
    side_of = chip // 2
    mate = chip + 1 - 2 * (chip % 2)
    owner = (chip > 0) & (chip < chips - 1)
    home = row * OWNERS + side_of

    def place(k):
        other = lax.rem(me + k, total)
        return (other // chips, lax.rem(other, chips) * CORES + core)

    greet([place(k) for k in range(1, total)] + [partner])

    window = pltpu.make_async_copy(
        coef_ref.at[:, pl.ds(0, window_ref.shape[1])], window_ref, l_sem.at[4]
    )

    def z_copy(route, h, device):
        return remote(
            first_rows.at[h] if routes[route][0] == 1 else raw[route - 2, h],
            raw[route, h],
            z_send.at[route, h],
            z_recv.at[route, h],
            device,
        )

    def inside(where):
        return (where >= 0) & (where < chips)

    def towards(route, h):
        d, s = routes[route]
        there = chip + s
        valid = inside(there) & inside(chip - s * (d - 1))
        if d == 1 and h == SPLIT - 1:
            valid = valid & inside(there + s)
        return there, valid

    def origin(route):
        d, s = routes[route]
        there = chip - s * d
        return there, inside(there)

    tiles = own.shape[0]

    def every(source_rows, target, sem, act):
        def some(index, carry):
            at = pl.ds(pl.multiple_of(index * tile, tile), tile)
            act(pltpu.make_async_copy(coef_ref.at[source_rows, at], target.at[index], sem))
            return carry

        lax.fori_loop(0, tiles, some, 0)

    def first_piece(h, act):
        start = pl.multiple_of(h * group + row * piece, piece)
        every(pl.ds(start, piece), first_rows.at[h], l_sem.at[5 + h], act)

    all_rows = pl.ds(0, orb_local)
    for h in range(SPLIT):
        first_piece(h, lambda copy: copy.start())
    id_copies = []
    for t in range(1, rows):
        id_copies.append(
            remote(ids_ref, ids_v.at[t], i_send.at[t], i_recv.at[t], row_peers[t - 1])
        )
        id_copies[-1].start()

    for h in range(SPLIT):
        first_piece(h, lambda copy: copy.wait())
        for route in range(2):
            there, valid = towards(route, h)

            @pl.when(valid)
            def _():
                z_copy(route, h, (row, there * CORES + core)).start()

    every(all_rows, own, l_sem.at[0], lambda copy: copy.start())
    swap = remote(ints_ref, both.at[1], i_send.at[0], i_recv.at[0], partner)
    swap.start()
    bring = pltpu.make_async_copy(ints_ref, both.at[0], l_sem.at[2])
    bring.start()
    window.start()
    first = pltpu.make_async_copy(ids_ref, ids_s.at[0], l_sem.at[1])
    first.start()
    first.wait()
    for t in range(1, rows):
        id_copies[t - 1].wait()
        move = pltpu.make_async_copy(ids_v.at[t], ids_s.at[t], l_sem.at[1])
        move.start()
        move.wait()

    def take(source, targets, t):
        step = 8

        def some(block, carry):
            for k in range(step):
                slot = block * step + k
                at = pl.ds(pl.multiple_of(slot * tile, tile), tile)
                value = source[ids_s[t, 0, slot]]
                height = value.shape[0] // len(targets)
                for n, target in enumerate(targets):
                    target[:, at] = value[n * height : (n + 1) * height]
            return carry

        lax.fori_loop(0, count // step, some, 0)

    def band(from_row):
        return pl.ds(pl.multiple_of(from_row * piece, piece), piece)

    def spread(from_row, came, h, t, device):
        k = lax.rem(came + chips - chip, chips) - 1
        return remote(
            staged.at[k, h, t - 1],
            kept.at[came, h, band(from_row), :],
            p_send.at[k, h, t],
            p_recv.at[k, h, t],
            device,
        )

    direct = remote(
        kept.at[chip, SPLIT - 1],
        kept.at[chip, SPLIT - 1],
        q_send,
        q_recv,
        (row, mate * CORES + core),
    )

    def handout(came, h, k):
        to = lax.rem(home + k, owners)
        return remote(
            ready.at[came, h, to],
            parts.at[came, h, row, chip],
            x_send.at[came, h, k],
            x_recv.at[came, h, me],
            (to // OWNERS, (1 + lax.rem(to, OWNERS)) * CORES + core),
        )

    def keep(came, h):
        return pltpu.make_async_copy(
            ready.at[came, h, home], parts.at[came, h, row, chip], x_send.at[came, h, 0]
        )

    def product(came, h):
        def one(step, carry):
            side = step // blocks
            block = step - side * blocks
            slot = (core + side - 2 * core * side) * aux_local
            lhs = kept[came, h, :, pl.ds(pl.multiple_of(block * width, width), width)]
            at = pl.ds(pl.multiple_of(block * tile, tile), tile)
            rhs = both[side, :, at, :].reshape(aux_local * tile, width)
            result = lax.dot_general(
                lhs, rhs, (((1,), (1,)), ((), ())), preferred_element_type=jnp.float32
            )
            for p in range(aux_local):
                value = result[:, p * tile : (p + 1) * tile].astype(ready.dtype)
                ready[came, h, :, slot + p, :, at] = value.reshape(owners, part, tile)
            return carry

        lax.fori_loop(0, CORES * blocks, one, 0)

        @pl.when(owner)
        def _():
            keep(came, h).start()

        @pl.when(jnp.logical_not(owner))
        def _():
            handout(came, h, 0).start()

        for k in range(1, owners):
            handout(came, h, k).start()

    every(all_rows, own, l_sem.at[0], lambda copy: copy.wait())
    take(own, [kept.at[chip, h] for h in range(SPLIT)], 0)

    @pl.when(jnp.logical_not(owner))
    def _():
        direct.start()

    def pass_on(d):
        for h in range(SPLIT):
            for route in range(len(routes)):
                if routes[route][0] != d:
                    continue
                s = routes[route][1]
                came, valid = origin(route)
                special = d == 1 and h == SPLIT - 1

                @pl.when(valid & inside(chip + s) if special else valid)
                def _():
                    z_copy(route, h, partner).wait_recv()
                    if d + 1 < chips:
                        there, onward = towards(route + 2, h)

                        @pl.when(onward)
                        def _():
                            z_copy(route + 2, h, (row, there * CORES + core)).start()

                @pl.when(valid & (came != mate) if special else valid)
                def _():
                    k = lax.rem(came + chips - chip, chips) - 1
                    for t in range(1, rows):
                        take(raw[route, h], [staged.at[k, h, t - 1]], t)
                        spread(row, came, h, t, row_peers[rows - t - 1]).start()
                    take(raw[route, h], [kept.at[came, h, band(row), :]], 0)

    def multiply(d):
        for h in range(SPLIT):
            for route in range(len(routes)):
                if routes[route][0] != d:
                    continue
                came, valid = origin(route)
                special = d == 1 and h == SPLIT - 1

                @pl.when(valid & (came != mate) if special else valid)
                def _():
                    for t in range(1, rows):
                        source_row = lax.rem(row + t, rows)
                        spread(source_row, came, h, t, row_peers[0]).wait_recv()
                    product(came, h)

    def multiply_direct():
        remote(
            kept.at[mate, SPLIT - 1], kept.at[mate, SPLIT - 1], q_send, q_recv, partner
        ).wait_recv()
        product(mate, SPLIT - 1)

    def prepare():
        height = weight.shape[1]
        aux = metric_ref.shape[0]
        at = lax.broadcasted_iota(jnp.int32, (height, aux), 0)
        which = lax.broadcasted_iota(jnp.int32, (height, aux), 1)
        expand = jnp.where(at // part == which, 1.0, 0.0).astype(jnp.float32)
        left = lax.dot_general(
            expand,
            metric_ref[...],
            (((1,), (1,)), ((), ())),
            precision=lax.Precision.HIGHEST,
            preferred_element_type=jnp.float32,
        )
        wide = lax.dot_general(
            left,
            expand,
            (((1,), (1,)), ((), ())),
            precision=lax.Precision.HIGHEST,
            preferred_element_type=jnp.float32,
        )
        a = lax.broadcasted_iota(jnp.int32, (height, height), 0)
        b = lax.broadcasted_iota(jnp.int32, (height, height), 1)
        wide = jnp.where(a % part == b % part, wide, 0.0)
        high = wide.astype(weight.dtype)
        weight[0] = high
        weight[1] = (wide - high.astype(jnp.float32)).astype(weight.dtype)
        for r in range(rows):
            total_ref[r] = jnp.zeros(total_ref.shape[1:], jnp.float32)

    for d in range(1, chips):
        pass_on(d)
        if d == 1:
            bring.wait()
            swap.wait()
            for h in range(SPLIT):
                product(chip, h)
        if d == 2:

            @pl.when(owner)
            def _():
                direct.start()
                prepare()
                multiply_direct()

            multiply(1)

    multiply(2)

    @pl.when(jnp.logical_not(owner))
    def _():
        multiply_direct()

    multiply(3)

    def collect(came, h):
        def arrive(k, carry):
            source = lax.rem(me + k, total)
            remote(
                ready.at[came, h, 0],
                parts.at[came, h, source // chips, lax.rem(source, chips)],
                x_send.at[came, h, 0],
                x_recv.at[came, h, source],
                partner,
            ).wait_recv()
            return carry

        lax.fori_loop(1, total, arrive, 0)
        keep(came, h).wait()
        height = weight.shape[1]
        local = mixed.shape[2]
        for r in range(rows):
            value = parts[came, h, r].astype(jnp.float32).reshape(height, local)
            value = value.astype(mixed.dtype)
            result = jnp.dot(weight[0], value, preferred_element_type=jnp.float32)
            result = result + jnp.dot(weight[1], value, preferred_element_type=jnp.float32)
            mixed[r] = result.astype(mixed.dtype)
            crossed[r * local : (r + 1) * local, :] = value.T

        def add(r, carry):
            total_ref[r] += jnp.dot(
                crossed[...], mixed[r], preferred_element_type=jnp.float32
            )
            return carry

        lax.fori_loop(0, rows, add, 0)

    height = share.shape[0]
    half = height * OWNERS
    first_copies, second_copies, last_copies = [], [], []
    order = [lax.rem(row + t, rows) for t in range(1, rows)] + [row]
    near = 1 + side_of
    far = OWNERS - side_of
    for t, peer in enumerate(order):
        first_copies.append(
            remote(gram.at[peer], part0.at[peer], send0.at[t], recv0.at[t], partner)
        )
        if t < rows - 1:
            second_copies.append(
                remote(sum0.at[peer], part1.at[t], send1.at[t], recv1.at[t], (peer, orb))
            )
    third = remote(
        sum1.at[1 - side_of], part2, send2, recv2, (row, far * CORES + core)
    )

    def block(from_core, from_side):
        start = pl.multiple_of(from_core * half + from_side * height, height)
        return full.at[pl.ds(start, height), :]

    own_block = block(core, side_of)
    for n, device in enumerate(
        [
            (row, far * CORES + core),
            (row, mate * CORES + core),
            (row, (chips - 1 - mate) * CORES + core),
        ]
    ):
        last_copies.append(
            remote(share, own_block, send3.at[n], recv3.at[0, side_of], device)
        )
    last_copies.append(remote(share, own_block, send3.at[3], recv3.at[1, side_of], partner))

    def relay(side, n):
        return remote(
            block(core, side), block(core, side), send3.at[n], recv3.at[1, side], partner
        )

    def landed(from_core, side, kind):
        remote(
            share, block(from_core, side), send3.at[0], recv3.at[kind, side], partner
        ).wait_recv()

    mine_half = pl.ds(pl.multiple_of(core * half, half), half)
    other_half = pl.ds(pl.multiple_of((1 - core) * half, half), half)

    @pl.when(owner)
    def _():
        def early(u, carry):
            collect(1 + u // SPLIT, lax.rem(u, SPLIT))
            return carry

        def late(u, carry):
            collect((chips - 1) * (1 - lax.rem(u, 2)), u // 2)
            return carry

        lax.fori_loop(0, OWNERS * SPLIT, early, 0)
        lax.fori_loop(0, 2 * SPLIT, late, 0)
        for t, peer in enumerate(order):
            gram[peer] = total_ref[peer, other_half].astype(gram.dtype)
            first_copies[t].start()
        for t, peer in enumerate(order):
            first_copies[t].wait_recv()
            value = total_ref[peer, mine_half] + part0[peer].astype(jnp.float32)
            sum0[peer] = value.astype(sum0.dtype)
            if t < rows - 1:
                second_copies[t].start()
        for copy in second_copies:
            copy.wait_recv()
        value = sum0[row].astype(jnp.float32)
        for t in range(rows - 1):
            value = value + part1[t].astype(jnp.float32)
        sum1[...] = value.astype(sum1.dtype).reshape(sum1.shape)
        third.start()
        third.wait_recv()
        value = sum1[side_of].astype(jnp.float32) + part2[...].astype(jnp.float32)
        share[...] = value.astype(share.dtype)
        for copy in last_copies:
            copy.start()
        start = pl.multiple_of(core * half + side_of * height, height)
        full[pl.ds(start, height), :] = share[...]
        landed(core, 1 - side_of, 0)
        relay(1 - side_of, 4).start()

    @pl.when(jnp.logical_not(owner))
    def _():
        landed(core, side_of, 0)
        relay(side_of, 4).start()
        landed(core, 1 - side_of, 0)
        relay(1 - side_of, 5).start()

    window.wait()
    result = jnp.dot(
        window_ref[:, mine_half], full[mine_half, :], preferred_element_type=jnp.float32
    )
    for side in range(OWNERS):
        landed(1 - core, side, 1)
    out_ref[...] = result + jnp.dot(
        window_ref[:, other_half], full[other_half, :], preferred_element_type=jnp.float32
    )

    @pl.when(owner)
    def _():
        for copy in first_copies + second_copies + [third] + last_copies:
            copy.wait_send()
        relay(1 - side_of, 4).wait_send()

    @pl.when(jnp.logical_not(owner))
    def _():
        relay(side_of, 4).wait_send()
        relay(1 - side_of, 5).wait_send()

    direct.wait_send()
    for route in range(len(routes)):
        d = routes[route][0]
        came, valid = origin(route)
        for h in range(SPLIT):
            there, sent = towards(route, h)
            special = d == 1 and h == SPLIT - 1

            @pl.when(sent)
            def _():
                z_copy(route, h, (row, there * CORES + core)).wait_send()

            @pl.when(valid & (came != mate) if special else valid)
            def _():
                for t in range(1, rows):
                    spread(row, came, h, t, row_peers[rows - t - 1]).wait_send()

    for came in range(chips):
        for h in range(SPLIT):

            @pl.when(jnp.logical_not(owner))
            def _():
                handout(came, h, 0).wait_send()

            for k in range(1, owners):
                handout(came, h, k).wait_send()


def exchange(integrals, ids, coefficients, metric, rows, orbs, blocks, count):
    chips = orbs // CORES
    orb_local, basis = coefficients.shape
    aux_local, local_rows, _ = integrals.shape
    tile = local_rows // blocks
    owners = rows * OWNERS
    piece = orb_local // rows // SPLIT
    group = piece * rows
    part = group // owners
    aux = aux_local * orbs
    window = local_rows * rows
    half = window // CORES
    height = half // OWNERS
    routes = 2 * (chips - 1)
    dtype = coefficients.dtype
    scratch = [
        pltpu.VMEM((basis // tile, piece, tile), dtype) for _ in range(routes * SPLIT)
    ]
    scratch += [
        pltpu.VMEM((basis // tile, orb_local, tile), dtype),
        pltpu.VMEM((SPLIT, basis // tile, piece, tile), dtype),
        pltpu.VMEM((chips, SPLIT, group, count * tile), dtype),
        pltpu.VMEM((chips - 1, SPLIT, rows - 1, piece, count * tile), dtype),
        pltpu.VMEM((CORES,) + integrals.shape, dtype),
        pltpu.VMEM((chips, SPLIT, owners, CORES * aux_local, part, local_rows), dtype),
        pltpu.VMEM((rows, 1, ids.shape[1]), jnp.int32),
        pltpu.SMEM((rows, 1, ids.shape[1]), jnp.int32),
        pltpu.VMEM((chips, SPLIT, rows, chips, CORES * aux_local, part, local_rows), dtype),
        pltpu.VMEM((2, aux * part, aux * part), dtype),
        pltpu.VMEM((window, aux * part), dtype),
        pltpu.VMEM((rows, aux * part, local_rows), dtype),
        pltpu.VMEM((rows, window, local_rows), jnp.float32),
        pltpu.VMEM((rows, half, local_rows), dtype),
        pltpu.VMEM((rows, half, local_rows), dtype),
        pltpu.VMEM((rows, half, local_rows), dtype),
        pltpu.VMEM((rows - 1, half, local_rows), dtype),
        pltpu.VMEM((OWNERS, height, local_rows), dtype),
        pltpu.VMEM((height, local_rows), dtype),
        pltpu.VMEM((height, local_rows), dtype),
        pltpu.VMEM((window, local_rows), dtype),
        pltpu.VMEM((orb_local, window), dtype),
        pltpu.SemaphoreType.DMA((routes, SPLIT)),
        pltpu.SemaphoreType.DMA((routes, SPLIT)),
        pltpu.SemaphoreType.DMA((chips - 1, SPLIT, rows)),
        pltpu.SemaphoreType.DMA((chips - 1, SPLIT, rows)),
        pltpu.SemaphoreType.DMA((5 + SPLIT,)),
        pltpu.SemaphoreType.DMA((rows,)),
        pltpu.SemaphoreType.DMA((rows,)),
        pltpu.SemaphoreType.DMA((chips, SPLIT, owners)),
        pltpu.SemaphoreType.DMA((chips, SPLIT, rows * chips)),
        pltpu.SemaphoreType.DMA,
        pltpu.SemaphoreType.DMA,
        pltpu.SemaphoreType.DMA((rows,)),
        pltpu.SemaphoreType.DMA((rows,)),
        pltpu.SemaphoreType.DMA((rows,)),
        pltpu.SemaphoreType.DMA((rows,)),
        pltpu.SemaphoreType.DMA,
        pltpu.SemaphoreType.DMA,
        pltpu.SemaphoreType.DMA((6,)),
        pltpu.SemaphoreType.DMA((2, OWNERS)),
    ]
    dims = (rows, chips, orb_local, tile, count, aux_local, blocks, part)
    return pl.pallas_call(
        functools.partial(exchange_kernel, dims),
        out_shape=jax.ShapeDtypeStruct((orb_local, local_rows), jnp.float32),
        in_specs=[pl.BlockSpec(memory_space=pltpu.VMEM)] * 2
        + [pl.BlockSpec(memory_space=pl.ANY)] * 2,
        out_specs=pl.BlockSpec(memory_space=pltpu.VMEM),
        scratch_shapes=scratch,
        compiler_params=pltpu.CompilerParams(
            collective_id=0, has_side_effects=True, vmem_limit_bytes=63 << 20
        ),
    )(ids, metric, coefficients, integrals)


def per_device(rows, orbs, integrals, tile_ids, coefficients, metric):
    orb_local, basis_width = coefficients.shape
    block_count, kept_count = tile_ids.shape
    chips = orbs // CORES
    if (
        chips != 2 * OWNERS
        or orb_local % (16 * SPLIT * rows)
        or orb_local % (8 * SPLIT * OWNERS * rows)
        or block_count * kept_count % 8
    ):
        return plain_device(rows, orbs, integrals, tile_ids, coefficients, metric)
    count = block_count * kept_count
    lanes = -(-count // 128) * 128
    ids = jnp.pad(tile_ids.reshape(1, count), ((0, 0), (0, lanes - count)))
    return exchange(integrals, ids, coefficients, metric, rows, orbs, block_count, count)


def plain_device(rows, orbs, integrals, tile_ids, coefficients, metric):
    aux_local, local_rows, kept_width = integrals.shape
    orb_local, basis_width = coefficients.shape
    block_count, kept_count = tile_ids.shape
    tile_rows = local_rows // block_count
    orbitals = orb_local * orbs
    aux = aux_local * orbs
    window = local_rows * rows
    part = orbitals // (rows * orbs)
    picked = pick(coefficients, tile_ids.reshape(block_count * kept_count), tile_rows)
    col_piece = lax.all_gather(picked, "orb", axis=0, tiled=True)
    slabs = integrals.reshape(aux_local, block_count, tile_rows, kept_width)
    halves = [
        jnp.einsum(
            "pmk,jk->pjm",
            slabs[:, b],
            col_piece[:, b * kept_width : (b + 1) * kept_width],
            preferred_element_type=jnp.float32,
        ).astype(jnp.bfloat16)
        for b in range(block_count)
    ]
    halves = jnp.concatenate(halves, axis=2)
    outgoing = halves.reshape(aux_local, rows * orbs, part, local_rows).transpose(1, 0, 2, 3)
    by_part = lax.all_to_all(outgoing, ("row", "orb"), split_axis=0, concat_axis=0, tiled=True)
    by_part = by_part.reshape(rows, aux, part, local_rows)
    mixed = jnp.einsum(
        "pq,rpjm->rqjm", metric, by_part.astype(jnp.float32), precision=lax.Precision.HIGHEST
    ).astype(jnp.bfloat16)
    gram = jnp.einsum(
        "rqjm,sqjn->rmsn", by_part, mixed, preferred_element_type=jnp.float32
    ).astype(jnp.bfloat16)
    gram = gram.reshape(orbs, window // orbs, rows, local_rows).transpose(2, 0, 1, 3)
    gram = gram.reshape(rows * window, local_rows)
    share = lax.psum_scatter(gram, ("row", "orb"), scatter_dimension=0, tiled=True)
    columns = lax.all_gather(share, "orb", axis=0, tiled=True)
    return jnp.dot(coefficients[:, :window], columns, preferred_element_type=jnp.float32)


def solution(mesh):
    return jax.shard_map(
        functools.partial(per_device, mesh.shape["row"], mesh.shape["orb"]),
        mesh=mesh,
        in_specs=(P("orb", "row", None), P("row", None), P("orb", None), P()),
        out_specs=P("orb", "row"),
        check_vma=False,
    )
```

time: 180 us -> 178 us (0.989)
  matrix products: 6.64 us -> 0 us
  Pallas kernels: 168 us -> 174 us
    dot_general x2 -> x0, matrix products: 6.64 us -> none  [the longest x1 3.41 us: per_device(): jnp.einsum('pq,rpjm->rqjm', order, by_part.astype(jnp.float32), precision...]
    pallas_call x2 -> x1, Pallas kernels: 168 us -> 174 us  [exchange(): pl.pallas_call(functools.partial(exchange_kernel, dims), out_shape=jax.Sh...]
where the time goes in v1:
time: 178 us; the launch traced here: 177 us
  Pallas kernels  174 us (98%)
  local copies, waits for them, and re-layouts  2.84 us (2%)
    pallas_call x1, Pallas kernels, exchange(): pl.pallas_call(functools.partial(exchange_kernel, dims), out_shape=jax.Sh...  174 us

profile of v1, /device:TPU:1, one launch (start us, length us, event | category | flops | bytes accessed | tf_op | source)
XLA Modules:
  0.0 177.3 jit_solution(5100225504062499270)
XLA Ops:
  0.0 0.8 reshape.3
  0.8 0.5 pad.4.ids_ref
  1.3 174.5 %shard_map.46 = f32[128,256]{1,0:T(8,128)} custom-call(s32[1,128]{1,0:T(1,128)} %pad.4.ids_ref, f32[24,24]{1,0:T(8,128)} %metric_ref.1, bf16[128,16384]{1,0:T(8,128)(2,1)} %coef_ref.1, bf16[3,256,5120]{2,1,0:T(8,128)(2,1)} %ints_ref.1), custom_call_target="tpu_custom_call" | custom-call | tf_op jit(solution)/shard_map/pallas_call | solution.py:599
  175.7 1.6 copy.6

commit v2 on v1

--- a/solution.py
+++ b/solution.py
@@ -67,12 +67,13 @@
     for route in range(len(routes)):
         for h in range(SPLIT):
             raw[route, h] = scratch.pop(0)
-    own, first_rows, kept, staged, both, ready, ids_v, ids_s = scratch[:8]
-    parts, weight, crossed, mixed, total_ref = scratch[8:13]
-    gram, part0, sum0, part1, sum1, part2, share, full, window_ref = scratch[13:22]
-    z_send, z_recv, p_send, p_recv, l_sem, i_send, i_recv, x_send, x_recv = scratch[22:31]
-    q_send, q_recv = scratch[31:33]
-    send0, recv0, send1, recv1, send2, recv2, send3, recv3 = scratch[33:]
+    own, kept, staged, both, ready, ids_v, ids_s = scratch[:7]
+    first_rows = scratch.pop()
+    parts, weight, crossed, mixed, total_ref = scratch[7:12]
+    gram, part0, sum0, part1, sum1, part2, share, full, window_ref = scratch[12:21]
+    z_send, z_recv, p_send, p_recv, l_sem, i_send, i_recv, x_send, x_recv = scratch[21:30]
+    q_send, q_recv, relayed, y_recv, y_send = scratch[30:35]
+    send0, recv0, send1, recv1, send2, recv2, send3, recv3 = scratch[35:]
     width = count * tile // blocks
     total = rows * chips
     owners = rows * OWNERS
@@ -126,12 +127,16 @@
     tiles = own.shape[0]
 
     def every(source_rows, target, sem, act):
+        step = 8
+
         def some(index, carry):
-            at = pl.ds(pl.multiple_of(index * tile, tile), tile)
-            act(pltpu.make_async_copy(coef_ref.at[source_rows, at], target.at[index], sem))
+            for n in range(step):
+                which = index * step + n
+                at = pl.ds(pl.multiple_of(which * tile, tile), tile)
+                act(pltpu.make_async_copy(coef_ref.at[source_rows, at], target.at[which], sem))
             return carry
 
-        lax.fori_loop(0, tiles, some, 0)
+        lax.fori_loop(0, tiles // step, some, 0)
 
     def first_piece(h, act):
         start = pl.multiple_of(h * group + row * piece, piece)
@@ -140,6 +145,20 @@
     all_rows = pl.ds(0, orb_local)
     for h in range(SPLIT):
         first_piece(h, lambda copy: copy.start())
+    bring = pltpu.make_async_copy(ints_ref, both.at[0], l_sem.at[2])
+    swap = remote(ints_ref, both.at[1], i_send.at[0], i_recv.at[0], partner)
+    for h in range(SPLIT):
+        first_piece(h, lambda copy: copy.wait())
+        for route in range(2):
+            there, valid = towards(route, h)
+
+            @pl.when(valid)
+            def _():
+                z_copy(route, h, (row, there * CORES + core)).start()
+
+    every(all_rows, own, l_sem.at[0], lambda copy: copy.start())
+    bring.start()
+    swap.start()
     id_copies = []
     for t in range(1, rows):
         id_copies.append(
@@ -147,20 +166,6 @@
         )
         id_copies[-1].start()
 
-    for h in range(SPLIT):
-        first_piece(h, lambda copy: copy.wait())
-        for route in range(2):
-            there, valid = towards(route, h)
-
-            @pl.when(valid)
-            def _():
-                z_copy(route, h, (row, there * CORES + core)).start()
-
-    every(all_rows, own, l_sem.at[0], lambda copy: copy.start())
-    swap = remote(ints_ref, both.at[1], i_send.at[0], i_recv.at[0], partner)
-    swap.start()
-    bring = pltpu.make_async_copy(ints_ref, both.at[0], l_sem.at[2])
-    bring.start()
     window.start()
     first = pltpu.make_async_copy(ids_ref, ids_s.at[0], l_sem.at[1])
     first.start()
@@ -207,49 +212,120 @@
         (row, mate * CORES + core),
     )
 
-    def handout(came, h, k):
+    whole = pl.ds(0, CORES * aux_local)
+
+    def handout(came, h, k, some=whole):
         to = lax.rem(home + k, owners)
         return remote(
-            ready.at[came, h, to],
-            parts.at[came, h, row, chip],
+            ready.at[came, h, to, some],
+            parts.at[came, h, row, chip, some],
             x_send.at[came, h, k],
             x_recv.at[came, h, me],
             (to // OWNERS, (1 + lax.rem(to, OWNERS)) * CORES + core),
         )
 
-    def keep(came, h):
+    def keep(came, h, some=whole):
         return pltpu.make_async_copy(
-            ready.at[came, h, home], parts.at[came, h, row, chip], x_send.at[came, h, 0]
-        )
+            ready.at[came, h, home, some],
+            parts.at[came, h, row, chip, some],
+            x_send.at[came, h, 0],
+        )
+
+    def along(came, h, side, some=whole):
+        return remote(
+            ready.at[came, h, row * OWNERS + side, some],
+            parts.at[came, h, row, chip, some],
+            x_send.at[came, h, side],
+            x_recv.at[came, h, me],
+            (row, (1 + side) * CORES + core),
+        )
+
+    def across(came, h, t, some=whole):
+        to = lax.rem(row + t, rows)
+        return remote(
+            ready.at[came, h, pl.ds(to * OWNERS, OWNERS), some],
+            relayed.at[came, h, t - 1, :, some],
+            x_send.at[came, h, OWNERS + t],
+            y_recv.at[came, h, t - 1],
+            (to, orb),
+        )
+
+    def onwards(came, h, t, side):
+        source = lax.rem(row + rows - t, rows)
+        return remote(
+            relayed.at[came, h, t - 1, side],
+            parts.at[came, h, source, chip],
+            y_send.at[came, h, t - 1, side],
+            x_recv.at[came, h, source * chips + chip],
+            (row, (1 + side) * CORES + core),
+        )
+
+    def hand(came, h, some=whole):
+        @pl.when(owner)
+        def _():
+            keep(came, h, some).start()
+            for k in range(1, owners):
+                handout(came, h, k, some).start()
+
+        @pl.when(jnp.logical_not(owner))
+        def _():
+            for t in range(1, rows):
+                across(came, h, t, some).start()
+            for side in range(OWNERS):
+                along(came, h, side, some).start()
+
+    def forward(came, h):
+        for t in range(1, rows):
+            across(came, h, t).wait_recv()
+            for side in range(OWNERS):
+                onwards(came, h, t, side).start()
+
+    def slot_of(side):
+        return (core + side - 2 * core * side) * aux_local
+
+    def some_products(lhs_of, side, block, store):
+        lhs = lhs_of(pl.ds(pl.multiple_of(block * width, width), width))
+        at = pl.ds(pl.multiple_of(block * tile, tile), tile)
+        rhs = both[side, :, at, :].reshape(aux_local * tile, width)
+        result = lax.dot_general(
+            lhs, rhs, (((1,), (1,)), ((), ())), preferred_element_type=jnp.float32
+        )
+        for p in range(aux_local):
+            value = result[:, p * tile : (p + 1) * tile].astype(ready.dtype)
+            store(slot_of(side) + p, at, value)
 
     def product(came, h):
         def one(step, carry):
             side = step // blocks
-            block = step - side * blocks
-            slot = (core + side - 2 * core * side) * aux_local
-            lhs = kept[came, h, :, pl.ds(pl.multiple_of(block * width, width), width)]
-            at = pl.ds(pl.multiple_of(block * tile, tile), tile)
-            rhs = both[side, :, at, :].reshape(aux_local * tile, width)
-            result = lax.dot_general(
-                lhs, rhs, (((1,), (1,)), ((), ())), preferred_element_type=jnp.float32
+
+            def store(slot, at, value):
+                ready[came, h, :, slot, :, at] = value.reshape(owners, part, tile)
+
+            some_products(
+                lambda at: kept[came, h, :, at], side, step - side * blocks, store
             )
-            for p in range(aux_local):
-                value = result[:, p * tile : (p + 1) * tile].astype(ready.dtype)
-                ready[came, h, :, slot + p, :, at] = value.reshape(owners, part, tile)
             return carry
 
         lax.fori_loop(0, CORES * blocks, one, 0)
 
-        @pl.when(owner)
-        def _():
-            keep(came, h).start()
-
-        @pl.when(jnp.logical_not(owner))
-        def _():
-            handout(came, h, 0).start()
-
-        for k in range(1, owners):
-            handout(came, h, k).start()
+        hand(came, h)
+
+    def own_product(side):
+        def one(block, carry):
+            def store(slot, at, value):
+                for h in range(SPLIT):
+                    rows_of_h = value[h * group : (h + 1) * group]
+                    ready[chip, h, :, slot, :, at] = rows_of_h.reshape(owners, part, tile)
+
+            some_products(
+                lambda at: kept[chip, :, :, at].reshape(orb_local, width), side, block, store
+            )
+            return carry
+
+        lax.fori_loop(0, blocks, one, 0)
+        some = pl.ds(slot_of(side), aux_local)
+        for h in range(SPLIT):
+            hand(chip, h, some)
 
     every(all_rows, own, l_sem.at[0], lambda copy: copy.wait())
     take(own, [kept.at[chip, h] for h in range(SPLIT)], 0)
@@ -285,8 +361,8 @@
                         spread(row, came, h, t, row_peers[rows - t - 1]).start()
                     take(raw[route, h], [kept.at[came, h, band(row), :]], 0)
 
-    def multiply(d):
-        for h in range(SPLIT):
+    def multiply(d, pieces=range(SPLIT)):
+        for h in pieces:
             for route in range(len(routes)):
                 if routes[route][0] != d:
                     continue
@@ -335,30 +411,50 @@
         for r in range(rows):
             total_ref[r] = jnp.zeros(total_ref.shape[1:], jnp.float32)
 
-    for d in range(1, chips):
-        pass_on(d)
-        if d == 1:
-            bring.wait()
-            swap.wait()
-            for h in range(SPLIT):
-                product(chip, h)
-        if d == 2:
-
-            @pl.when(owner)
-            def _():
-                direct.start()
-                prepare()
-                multiply_direct()
-
-            multiply(1)
+    bring.wait()
+    own_product(0)
+    pass_on(1)
+    swap.wait()
+    own_product(1)
+    pass_on(2)
+
+    @pl.when(owner)
+    def _():
+        direct.start()
+        prepare()
+
+    multiply(1)
+
+    @pl.when(owner)
+    def _():
+        multiply_direct()
+
+    pass_on(3)
+    end = jnp.logical_not(owner)
+    inward = 1 - 2 * side_of
+
+    @pl.when(end)
+    def _():
+        for h in range(SPLIT):
+            forward(chip, h)
+        forward(mate, 0)
 
     multiply(2)
-
-    @pl.when(jnp.logical_not(owner))
-    def _():
+    multiply(3, [0])
+
+    @pl.when(end)
+    def _():
+        for h in range(SPLIT):
+            forward(chip + 2 * inward, h)
         multiply_direct()
-
-    multiply(3)
+        forward(chip + 3 * inward, 0)
+
+    multiply(3, [1])
+
+    @pl.when(end)
+    def _():
+        forward(mate, SPLIT - 1)
+        forward(chip + 3 * inward, SPLIT - 1)
 
     def collect(came, h):
         def arrive(k, carry):
@@ -442,16 +538,17 @@
 
     @pl.when(owner)
     def _():
-        def early(u, carry):
-            collect(1 + u // SPLIT, lax.rem(u, SPLIT))
+        def inner(u, carry):
+            collect(1 + lax.rem(u, 2), u // 2)
             return carry
 
-        def late(u, carry):
-            collect((chips - 1) * (1 - lax.rem(u, 2)), u // 2)
+        def outer(u, carry):
+            collect((chips - 1) * lax.rem(u, 2), u // 2)
             return carry
 
-        lax.fori_loop(0, OWNERS * SPLIT, early, 0)
-        lax.fori_loop(0, 2 * SPLIT, late, 0)
+        for h in range(SPLIT):
+            lax.fori_loop(h * OWNERS, (h + 1) * OWNERS, inner, 0)
+            lax.fori_loop(h * OWNERS, (h + 1) * OWNERS, outer, 0)
         for t, peer in enumerate(order):
             gram[peer] = total_ref[peer, other_half].astype(gram.dtype)
             first_copies[t].start()
@@ -526,12 +623,19 @@
     for came in range(chips):
         for h in range(SPLIT):
 
+            @pl.when(owner)
+            def _():
+                for k in range(1, owners):
+                    handout(came, h, k).wait_send()
+
             @pl.when(jnp.logical_not(owner))
             def _():
-                handout(came, h, 0).wait_send()
-
-            for k in range(1, owners):
-                handout(came, h, k).wait_send()
+                for side in range(OWNERS):
+                    along(came, h, side).wait_send()
+                for t in range(1, rows):
+                    across(came, h, t).wait_send()
+                    for side in range(OWNERS):
+                        onwards(came, h, t, side).wait_send()
 
 
 def exchange(integrals, ids, coefficients, metric, rows, orbs, blocks, count):
@@ -554,7 +658,6 @@
     ]
     scratch += [
         pltpu.VMEM((basis // tile, orb_local, tile), dtype),
-        pltpu.VMEM((SPLIT, basis // tile, piece, tile), dtype),
         pltpu.VMEM((chips, SPLIT, group, count * tile), dtype),
         pltpu.VMEM((chips - 1, SPLIT, rows - 1, piece, count * tile), dtype),
         pltpu.VMEM((CORES,) + integrals.shape, dtype),
@@ -586,6 +689,11 @@
         pltpu.SemaphoreType.DMA((chips, SPLIT, rows * chips)),
         pltpu.SemaphoreType.DMA,
         pltpu.SemaphoreType.DMA,
+        pltpu.VMEM(
+            (chips, SPLIT, rows - 1, OWNERS, CORES * aux_local, part, local_rows), dtype
+        ),
+        pltpu.SemaphoreType.DMA((chips, SPLIT, rows - 1)),
+        pltpu.SemaphoreType.DMA((chips, SPLIT, rows - 1, OWNERS)),
         pltpu.SemaphoreType.DMA((rows,)),
         pltpu.SemaphoreType.DMA((rows,)),
         pltpu.SemaphoreType.DMA((rows,)),
@@ -594,6 +702,7 @@
         pltpu.SemaphoreType.DMA,
         pltpu.SemaphoreType.DMA((6,)),
         pltpu.SemaphoreType.DMA((2, OWNERS)),
+        pltpu.VMEM((SPLIT, basis // tile, piece, tile), dtype),
     ]
     dims = (rows, chips, orb_local, tile, count, aux_local, blocks, part)
     return pl.pallas_call(
@@ -618,6 +727,7 @@
         or orb_local % (16 * SPLIT * rows)
         or orb_local % (8 * SPLIT * OWNERS * rows)
         or block_count * kept_count % 8
+        or basis_width // (integrals.shape[1] // block_count) % 8
     ):
         return plain_device(rows, orbs, integrals, tile_ids, coefficients, metric)
     count = block_count * kept_count

time: 178 us -> 161 us (0.904)
  Pallas kernels: 174 us -> 158 us
    pallas_call x1, Pallas kernels: 174 us -> 158 us  [exchange(): pl.pallas_call(functools.partial(exchange_kernel, dims), out_shape=jax.Sh...]
where the time goes in v2:
time: 161 us
  Pallas kernels  158 us (98%)
  local copies, waits for them, and re-layouts  2.84 us (2%)
    pallas_call x1, Pallas kernels, exchange(): pl.pallas_call(functools.partial(exchange_kernel, dims), out_shape=jax.Sh...  158 us

profile of v2, /device:TPU:1, one launch (start us, length us, event | category | flops | bytes accessed | tf_op | source)
XLA Modules:
  0.0 161.2 jit_solution(11497962406155868905)
XLA Ops:
  0.0 0.8 reshape.3
  0.8 0.5 pad.4.ids_ref
  1.3 158.3 %shard_map.46 = f32[128,256]{1,0:T(8,128)} custom-call(s32[1,128]{1,0:T(1,128)} %pad.4.ids_ref, f32[24,24]{1,0:T(8,128)} %metric_ref.1, bf16[128,16384]{1,0:T(8,128)(2,1)} %coef_ref.1, bf16[3,256,5120]{2,1,0:T(8,128)(2,1)} %ints_ref.1), custom_call_target="tpu_custom_call" | custom-call | tf_op jit(solution)/shard_map/pallas_call | solution.py:708
  159.6 1.6 copy.6

commit v3 on v2

--- a/solution.py
+++ b/solution.py
@@ -69,6 +69,8 @@
             raw[route, h] = scratch.pop(0)
     own, kept, staged, both, ready, ids_v, ids_s = scratch[:7]
     first_rows = scratch.pop()
+    partz, sumz, partb, sendz, recvz, sendb, recvb = scratch[-7:]
+    scratch = scratch[:-7]
     parts, weight, crossed, mixed, total_ref = scratch[7:12]
     gram, part0, sum0, part1, sum1, part2, share, full, window_ref = scratch[12:21]
     z_send, z_recv, p_send, p_recv, l_sem, i_send, i_recv, x_send, x_recv = scratch[21:30]
@@ -490,7 +492,9 @@
 
     height = share.shape[0]
     half = height * OWNERS
+    quarter = height // 2
     first_copies, second_copies, last_copies = [], [], []
+    across_copies, after_copies = [], []
     order = [lax.rem(row + t, rows) for t in range(1, rows)] + [row]
     near = 1 + side_of
     far = OWNERS - side_of
@@ -498,9 +502,31 @@
         first_copies.append(
             remote(gram.at[peer], part0.at[peer], send0.at[t], recv0.at[t], partner)
         )
+        start = pl.multiple_of((1 - side_of) * height + quarter, quarter)
+        across_copies.append(
+            remote(
+                sum0.at[peer, pl.ds(start, quarter)],
+                partz.at[peer],
+                sendz.at[t],
+                recvz.at[t],
+                (row, far * CORES + core),
+            )
+        )
         if t < rows - 1:
             second_copies.append(
-                remote(sum0.at[peer], part1.at[t], send1.at[t], recv1.at[t], (peer, orb))
+                [
+                    remote(
+                        sum0.at[peer, pl.ds(side * height, quarter)],
+                        part1.at[t, side],
+                        send1.at[t, side],
+                        recv1.at[t, side],
+                        (peer, orb),
+                    )
+                    for side in range(OWNERS)
+                ]
+            )
+            after_copies.append(
+                remote(sumz.at[peer], partb.at[t], sendb.at[t], recvb.at[t], (peer, orb))
             )
     third = remote(
         sum1.at[1 - side_of], part2, send2, recv2, (row, far * CORES + core)
@@ -556,18 +582,35 @@
             first_copies[t].wait_recv()
             value = total_ref[peer, mine_half] + part0[peer].astype(jnp.float32)
             sum0[peer] = value.astype(sum0.dtype)
+            across_copies[t].start()
             if t < rows - 1:
-                second_copies[t].start()
-        for copy in second_copies:
+                for copy in second_copies[t]:
+                    copy.start()
+        for t, peer in enumerate(order):
+            across_copies[t].wait_recv()
+            start = pl.multiple_of(side_of * height + quarter, quarter)
+            value = sum0[peer, pl.ds(start, quarter)].astype(jnp.float32)
+            sumz[peer] = (value + partz[peer].astype(jnp.float32)).astype(sumz.dtype)
+            if t < rows - 1:
+                after_copies[t].start()
+        for copies in second_copies:
+            for copy in copies:
+                copy.wait_recv()
+        for side in range(OWNERS):
+            value = sum0[row, side * height : side * height + quarter].astype(jnp.float32)
+            for t in range(rows - 1):
+                value = value + part1[t, side].astype(jnp.float32)
+            sum1[side] = value.astype(sum1.dtype)
+        third.start()
+        for copy in after_copies:
             copy.wait_recv()
-        value = sum0[row].astype(jnp.float32)
+        value = sumz[row].astype(jnp.float32)
         for t in range(rows - 1):
-            value = value + part1[t].astype(jnp.float32)
-        sum1[...] = value.astype(sum1.dtype).reshape(sum1.shape)
-        third.start()
+            value = value + partb[t].astype(jnp.float32)
+        share[quarter:] = value.astype(share.dtype)
         third.wait_recv()
         value = sum1[side_of].astype(jnp.float32) + part2[...].astype(jnp.float32)
-        share[...] = value.astype(share.dtype)
+        share[:quarter] = value.astype(share.dtype)
         for copy in last_copies:
             copy.start()
         start = pl.multiple_of(core * half + side_of * height, height)
@@ -594,7 +637,9 @@
 
     @pl.when(owner)
     def _():
-        for copy in first_copies + second_copies + [third] + last_copies:
+        for copy in sum(second_copies, first_copies + across_copies + after_copies):
+            copy.wait_send()
+        for copy in [third] + last_copies:
             copy.wait_send()
         relay(1 - side_of, 4).wait_send()
 
@@ -651,6 +696,7 @@
     window = local_rows * rows
     half = window // CORES
     height = half // OWNERS
+    quarter = height // 2
     routes = 2 * (chips - 1)
     dtype = coefficients.dtype
     scratch = [
@@ -672,9 +718,9 @@
         pltpu.VMEM((rows, half, local_rows), dtype),
         pltpu.VMEM((rows, half, local_rows), dtype),
         pltpu.VMEM((rows, half, local_rows), dtype),
-        pltpu.VMEM((rows - 1, half, local_rows), dtype),
-        pltpu.VMEM((OWNERS, height, local_rows), dtype),
-        pltpu.VMEM((height, local_rows), dtype),
+        pltpu.VMEM((rows - 1, OWNERS, quarter, local_rows), dtype),
+        pltpu.VMEM((OWNERS, quarter, local_rows), dtype),
+        pltpu.VMEM((quarter, local_rows), dtype),
         pltpu.VMEM((height, local_rows), dtype),
         pltpu.VMEM((window, local_rows), dtype),
         pltpu.VMEM((orb_local, window), dtype),
@@ -696,12 +742,19 @@
         pltpu.SemaphoreType.DMA((chips, SPLIT, rows - 1, OWNERS)),
         pltpu.SemaphoreType.DMA((rows,)),
         pltpu.SemaphoreType.DMA((rows,)),
-        pltpu.SemaphoreType.DMA((rows,)),
-        pltpu.SemaphoreType.DMA((rows,)),
+        pltpu.SemaphoreType.DMA((rows, OWNERS)),
+        pltpu.SemaphoreType.DMA((rows, OWNERS)),
         pltpu.SemaphoreType.DMA,
         pltpu.SemaphoreType.DMA,
         pltpu.SemaphoreType.DMA((6,)),
         pltpu.SemaphoreType.DMA((2, OWNERS)),
+        pltpu.VMEM((rows, quarter, local_rows), dtype),
+        pltpu.VMEM((rows, quarter, local_rows), dtype),
+        pltpu.VMEM((rows - 1, quarter, local_rows), dtype),
+        pltpu.SemaphoreType.DMA((rows,)),
+        pltpu.SemaphoreType.DMA((rows,)),
+        pltpu.SemaphoreType.DMA((rows,)),
+        pltpu.SemaphoreType.DMA((rows,)),
         pltpu.VMEM((SPLIT, basis // tile, piece, tile), dtype),
     ]
     dims = (rows, chips, orb_local, tile, count, aux_local, blocks, part)

time: 161 us -> 155 us (0.963)
  Pallas kernels: 158 us -> 152 us
    pallas_call x1, Pallas kernels: 158 us -> 152 us  [exchange(): pl.pallas_call(functools.partial(exchange_kernel, dims), out_shape=jax.Sh...]
where the time goes in v3:
time: 155 us; the launch traced here: 154 us
  Pallas kernels  152 us (98%)
  local copies, waits for them, and re-layouts  2.84 us (2%)
    pallas_call x1, Pallas kernels, exchange(): pl.pallas_call(functools.partial(exchange_kernel, dims), out_shape=jax.Sh...  152 us

profile of v3, /device:TPU:1, one launch (start us, length us, event | category | flops | bytes accessed | tf_op | source)
XLA Modules:
  0.0 154.4 jit_solution(14463497787889979719)
XLA Ops:
  0.0 0.8 reshape.3
  0.8 0.5 pad.4.ids_ref
  1.3 151.6 %shard_map.46 = f32[128,256]{1,0:T(8,128)} custom-call(s32[1,128]{1,0:T(1,128)} %pad.4.ids_ref, f32[24,24]{1,0:T(8,128)} %metric_ref.1, bf16[128,16384]{1,0:T(8,128)(2,1)} %coef_ref.1, bf16[3,256,5120]{2,1,0:T(8,128)(2,1)} %ints_ref.1), custom_call_target="tpu_custom_call" | custom-call | tf_op jit(solution)/shard_map/pallas_call | solution.py:761
  152.8 1.6 %copy.6 = f32[128,256]{1,0:T(8,128)} copy(f32[128,256]{1,0:T(8,128)} %shard_map.46) | data formatting | bytes 262144

commit v4 on v3

--- a/solution.py
+++ b/solution.py
@@ -537,17 +537,29 @@
         return full.at[pl.ds(start, height), :]
 
     own_block = block(core, side_of)
-    for n, device in enumerate(
-        [
-            (row, far * CORES + core),
-            (row, mate * CORES + core),
-            (row, (chips - 1 - mate) * CORES + core),
-        ]
-    ):
+    targets = [
+        ((row, far * CORES + core), 0),
+        ((row, mate * CORES + core), 0),
+        ((row, (chips - 1 - mate) * CORES + core), 0),
+        (partner, 1),
+    ]
+    for n, (device, kind) in enumerate(targets):
         last_copies.append(
-            remote(share, own_block, send3.at[n], recv3.at[0, side_of], device)
-        )
-    last_copies.append(remote(share, own_block, send3.at[3], recv3.at[1, side_of], partner))
+            remote(share, own_block, send3.at[n], recv3.at[kind, side_of], device)
+        )
+
+    def publish(which):
+        at = which * quarter
+        start = core * half + side_of * height + at
+        target = full.at[pl.ds(pl.multiple_of(start, quarter), quarter), :]
+        for n, (device, kind) in enumerate(targets):
+            remote(
+                share.at[pl.ds(at, quarter)],
+                target,
+                send3.at[n],
+                recv3.at[kind, side_of],
+                device,
+            ).start()
 
     def relay(side, n):
         return remote(
@@ -608,11 +620,11 @@
         for t in range(rows - 1):
             value = value + partb[t].astype(jnp.float32)
         share[quarter:] = value.astype(share.dtype)
+        publish(1)
         third.wait_recv()
         value = sum1[side_of].astype(jnp.float32) + part2[...].astype(jnp.float32)
         share[:quarter] = value.astype(share.dtype)
-        for copy in last_copies:
-            copy.start()
+        publish(0)
         start = pl.multiple_of(core * half + side_of * height, height)
         full[pl.ds(start, height), :] = share[...]
         landed(core, 1 - side_of, 0)

time: 155 us -> 155 us (level)
  no operation moved by 1% of the time
where the time goes in v4:
time: 155 us; the launch traced here: 154 us
  Pallas kernels  151 us (97%)
  local copies, waits for them, and re-layouts  2.84 us (2%)
    pallas_call x1, Pallas kernels, exchange(): pl.pallas_call(functools.partial(exchange_kernel, dims), out_shape=jax.Sh...  151 us

profile of v4, /device:TPU:1, one launch (start us, length us, event | category | flops | bytes accessed | tf_op | source)
XLA Modules:
  0.0 154.2 jit_solution(9320467141446987901)
XLA Ops:
  0.0 0.8 reshape.3
  0.8 0.5 pad.4.ids_ref
  1.3 151.4 %shard_map.46 = f32[128,256]{1,0:T(8,128)} custom-call(s32[1,128]{1,0:T(1,128)} %pad.4.ids_ref, f32[24,24]{1,0:T(8,128)} %metric_ref.1, bf16[128,16384]{1,0:T(8,128)(2,1)} %coef_ref.1, bf16[3,256,5120]{2,1,0:T(8,128)(2,1)} %ints_ref.1), custom_call_target="tpu_custom_call" | custom-call | tf_op jit(solution)/shard_map/pallas_call | solution.py:773
  152.7 1.6 %copy.6 = f32[128,256]{1,0:T(8,128)} copy(f32[128,256]{1,0:T(8,128)} %shard_map.46) | data formatting | bytes 262144

commit v5 on v4

--- a/solution.py
+++ b/solution.py
@@ -439,15 +439,24 @@
     def _():
         for h in range(SPLIT):
             forward(chip, h)
+
+    multiply(2, [0])
+
+    @pl.when(end)
+    def _():
         forward(mate, 0)
 
-    multiply(2)
+    multiply(2, [1])
+
+    @pl.when(end)
+    def _():
+        forward(chip + 2 * inward, 0)
+
     multiply(3, [0])
 
     @pl.when(end)
     def _():
-        for h in range(SPLIT):
-            forward(chip + 2 * inward, h)
+        forward(chip + 2 * inward, 1)
         multiply_direct()
         forward(chip + 3 * inward, 0)
 

time: 155 us -> 158 us (1.019)
  Pallas kernels: 151 us -> 155 us
    pallas_call x1, Pallas kernels: 151 us -> 155 us  [exchange(): pl.pallas_call(functools.partial(exchange_kernel, dims), out_shape=jax.Sh...]
where the time goes in v5:
time: 158 us
  Pallas kernels  155 us (98%)
  local copies, waits for them, and re-layouts  2.84 us (2%)
    pallas_call x1, Pallas kernels, exchange(): pl.pallas_call(functools.partial(exchange_kernel, dims), out_shape=jax.Sh...  155 us

profile of v5, /device:TPU:1, one launch (start us, length us, event | category | flops | bytes accessed | tf_op | source)
XLA Modules:
  0.0 157.5 jit_solution(8357555134097362937)
XLA Ops:
  0.0 0.8 reshape.3
  0.8 0.5 pad.4.ids_ref
  1.3 154.7 %shard_map.46 = f32[128,256]{1,0:T(8,128)} custom-call(s32[1,128]{1,0:T(1,128)} %pad.4.ids_ref, f32[24,24]{1,0:T(8,128)} %metric_ref.1, bf16[128,16384]{1,0:T(8,128)(2,1)} %coef_ref.1, bf16[3,256,5120]{2,1,0:T(8,128)(2,1)} %ints_ref.1), custom_call_target="tpu_custom_call" | custom-call | tf_op jit(solution)/shard_map/pallas_call | solution.py:782
  155.9 1.6 copy.6

commit v6 on v4

--- a/solution.py
+++ b/solution.py
@@ -425,13 +425,6 @@
         direct.start()
         prepare()
 
-    multiply(1)
-
-    @pl.when(owner)
-    def _():
-        multiply_direct()
-
-    pass_on(3)
     end = jnp.logical_not(owner)
     inward = 1 - 2 * side_of
 
@@ -439,7 +432,18 @@
     def _():
         for h in range(SPLIT):
             forward(chip, h)
+
+    multiply(1)
+
+    @pl.when(owner)
+    def _():
+        multiply_direct()
+
+    @pl.when(end)
+    def _():
         forward(mate, 0)
+
+    pass_on(3)
 
     multiply(2)
     multiply(3, [0])

time: 155 us -> 157 us (1.013)
  Pallas kernels: 151 us -> 154 us
    pallas_call x1, Pallas kernels: 151 us -> 154 us  [exchange(): pl.pallas_call(functools.partial(exchange_kernel, dims), out_shape=jax.Sh...]
where the time goes in v6:
time: 157 us
  Pallas kernels  154 us (98%)
  local copies, waits for them, and re-layouts  2.84 us (2%)
    pallas_call x1, Pallas kernels, exchange(): pl.pallas_call(functools.partial(exchange_kernel, dims), out_shape=jax.Sh...  154 us

profile of v6, /device:TPU:1, one launch (start us, length us, event | category | flops | bytes accessed | tf_op | source)
XLA Modules:
  0.0 156.7 jit_solution(3573856466008395080)
XLA Ops:
  0.0 0.8 reshape.3
  0.8 0.5 pad.4.ids_ref
  1.3 153.8 %shard_map.46 = f32[128,256]{1,0:T(8,128)} custom-call(s32[1,128]{1,0:T(1,128)} %pad.4.ids_ref, f32[24,24]{1,0:T(8,128)} %metric_ref.1, bf16[128,16384]{1,0:T(8,128)(2,1)} %coef_ref.1, bf16[3,256,5120]{2,1,0:T(8,128)(2,1)} %ints_ref.1), custom_call_target="tpu_custom_call" | custom-call | tf_op jit(solution)/shard_map/pallas_call | solution.py:777
  155.1 1.6 %copy.6 = f32[128,256]{1,0:T(8,128)} copy(f32[128,256]{1,0:T(8,128)} %shard_map.46) | data formatting | bytes 262144
